TPU v7x, 256 devices: a whole 4x4x8 slice. The times are simulated.
256 devices in a mesh: wide: 32 (over y_lo, z, core), narrow: 8 (over x, y_hi).
Axes of the slice: x: 4, y: 4 (y_hi: 2, y_lo: 2; y = y_hi * 2 + y_lo), z: 8, core: 2. Of those that a mesh axis runs over, the one named last changes fastest.
Arguments:
- dark: bfloat16 [64, 32, 8, 16], P(None, None, 'narrow'), may hold values from -6 to 6
- w_enc: bfloat16 [27, 64, 64], replicated, may hold values from -0.15625 to 0.15625
- up_weight: bfloat16 [512, 16, 64], replicated, may hold values from -0.75 to 0.75
- w_dec: bfloat16 [27, 16, 16], replicated, may hold values from -0.3125 to 0.3125
- cotangent: bfloat16 [16, 256, 64, 128], P(None, 'wide', 'narrow'), may hold values from -6 to 6
Outputs:
- grad_dark: float32 [64, 32, 8, 16], P(None, None, 'narrow')
- grad_w_enc: float32 [27, 64, 64], replicated
- grad_up_weight: float32 [512, 16, 64], P(('wide', 'narrow'))
- grad_w_dec: float32 [27, 16, 16], replicated
All inputs are finite; a program needn't handle non-finite values.
Results may differ from a plain program's by a relative error of at most 0.0053.
Values may be sent and summed in bfloat16 or wider, within the bound.
A program may use at most 64 MiB of HBM per device.

v0:
```python
import math
import jax
import jax.numpy as jnp
from jax import lax
from jax.sharding import PartitionSpec as P

RATIO = 8


def padded_2(block, sides, width):
    for axis, dim in sides:
        count = lax.axis_size(axis)
        forward = [(i, i + 1) for i in range(count - 1)]
        backward = [(target, source) for source, target in forward]
        low = lax.ppermute(
            lax.slice_in_dim(block, block.shape[dim] - width, None, axis=dim), axis, forward
        )
        high = lax.ppermute(lax.slice_in_dim(block, 0, width, axis=dim), axis, backward)
        block = jnp.concatenate([low, block, high], axis=dim)
    return block


def silu_slope(values):
    sigma = jax.nn.sigmoid(values)
    return sigma * (1.0 + values * (1.0 - sigma))


def coarse_margin(field):
    return padded_2(field, (("narrow", 2),), 1)


def pad_coarse(field):
    return jnp.pad(field, ((0, 0), (1, 1), (0, 0), (1, 1)))


def pad_fine(field):
    return jnp.pad(field, ((0, 0), (0, 0), (0, 0), (1, 1)))


def flatten(kernel):
    return kernel.transpose(1, 0, 2).reshape(kernel.shape[1], -1)


def transposed(kernel):
    return kernel[::-1].transpose(2, 0, 1).reshape(kernel.shape[2], -1)


def unflatten(flat):
    return flat.reshape(flat.shape[0], 27, -1).transpose(1, 0, 2)


def columns(padded, first, count, depth, width):
    pieces = []
    for shift_x in range(3):
        for shift_z in range(3):
            for shift_y in range(3):
                pieces.append(
                    padded[
                        :,
                        first + shift_x : first + shift_x + count,
                        shift_z : shift_z + depth,
                        shift_y : shift_y + width,
                    ]
                )
    return jnp.concatenate(pieces, 0)


def block_size(planes):
    return planes // 4


def convolve_blocks(padded, flat):
    planes = padded.shape[1] - 2
    depth = padded.shape[2] - 2
    width = padded.shape[3] - 2
    block = block_size(planes)
    results = []
    for first in range(0, planes, block):
        stacked = columns(padded, first, block, depth, width)
        results.append(
            jnp.einsum("ok,kxzy->oxzy", flat, stacked, preferred_element_type=jnp.float32)
        )
    return jnp.concatenate(results, 1)


def upsample(table, enc_planes, ratio, fine_ch):
    chans = enc_planes.shape[0]
    planes = enc_planes.shape[1]
    depth = enc_planes.shape[2]
    width = enc_planes.shape[3]
    up_rows = jnp.dot(
        table, enc_planes.reshape(chans, planes * depth * width), preferred_element_type=jnp.float32
    )
    return (
        up_rows.reshape(ratio, ratio, ratio, fine_ch, planes, depth, width)
        .transpose(3, 4, 0, 5, 1, 6, 2)
        .reshape(fine_ch, planes * ratio, depth * ratio, width * ratio)
        .astype(jnp.bfloat16)
    )


def on_device(dark, w_enc, up_weight, w_dec, cotangent):
    ratio = RATIO
    chans = dark.shape[0]
    fine_ch = w_dec.shape[1]
    subs = up_weight.shape[0]
    wide_count = lax.axis_size("wide")
    narrow_count = lax.axis_size("narrow")
    coarse_planes = dark.shape[1]
    own_planes = coarse_planes // wide_count
    depth = dark.shape[2]
    width = dark.shape[3]
    first_plane = lax.axis_index("wide") * own_planes
    dark_padded = pad_coarse(coarse_margin(dark))
    enc_flat_kernel = flatten(w_enc)
    enc_pre = convolve_blocks(dark_padded, enc_flat_kernel)
    encoded = jax.nn.silu(enc_pre).astype(jnp.bfloat16)
    enc_window = lax.dynamic_slice_in_dim(
        jnp.pad(encoded, ((0, 0), (1, 1), (0, 0), (0, 0))), first_plane, own_planes + 2, 1
    )
    enc_own = enc_window[:, 1 : own_planes + 1]
    cells = own_planes * depth * width
    enc_flat = enc_own.reshape(chans, cells)
    table = up_weight.reshape(subs * fine_ch, chans)
    fine_planes = own_planes * ratio
    fine_depth = depth * ratio
    fine_width = width * ratio
    upsampled = upsample(table, enc_own, ratio, fine_ch)
    up_padded = pad_fine(padded_2(upsampled, (("wide", 1), ("narrow", 2)), 1))
    dec_flat = flatten(w_dec)
    cot_float = cotangent.astype(jnp.float32)
    block = block_size(fine_planes)
    grad_pieces = []
    dec_total = jnp.zeros((fine_ch, 27 * fine_ch), jnp.float32)
    for first in range(0, fine_planes, block):
        stacked = columns(up_padded, first, block, fine_depth, fine_width)
        pre_block = jnp.einsum(
            "ok,kxzy->oxzy", dec_flat, stacked, preferred_element_type=jnp.float32
        )
        piece = (cot_float[:, first : first + block] * silu_slope(pre_block)).astype(jnp.bfloat16)
        dec_total = dec_total + jnp.einsum(
            "oxzy,kxzy->ok", piece, stacked, preferred_element_type=jnp.float32
        )
        grad_pieces.append(piece)
    dec_grad = jnp.concatenate(grad_pieces, 1)
    grad_padded = pad_fine(padded_2(dec_grad, (("wide", 1), ("narrow", 2)), 1))
    back_up = convolve_blocks(grad_padded, transposed(w_dec))
    up_grad = (cot_float + back_up).astype(jnp.bfloat16)
    grad_rows = (
        up_grad.reshape(fine_ch, own_planes, ratio, depth, ratio, width, ratio)
        .transpose(2, 4, 6, 0, 1, 3, 5)
        .reshape(subs * fine_ch, cells)
    )
    enc_grad_own = (
        jnp.einsum("kc,kn->cn", table, grad_rows, preferred_element_type=jnp.float32)
        .reshape(chans, own_planes, depth, width)
        .astype(jnp.bfloat16)
    )
    enc_grad = lax.all_gather(enc_grad_own, "wide", axis=1, tiled=True)
    enc_pre_grad = (enc_grad.astype(jnp.float32) * silu_slope(enc_pre)).astype(jnp.bfloat16)
    grad_own = lax.dynamic_slice_in_dim(enc_pre_grad, first_plane, own_planes, 1)
    dark_own = lax.dynamic_slice_in_dim(dark_padded, first_plane, own_planes + 2, 1)
    stacked_own = columns(dark_own, 0, own_planes, depth, width)
    enc_total = jnp.einsum(
        "oxzy,kxzy->ok", grad_own, stacked_own, preferred_element_type=jnp.float32
    )
    grad_dark = convolve_blocks(pad_coarse(coarse_margin(enc_pre_grad)), transposed(w_enc))
    coarse_count = coarse_planes * depth * narrow_count * width
    coarse_scale = 1.0 / math.sqrt(coarse_count)
    fine_scale = 1.0 / math.sqrt(coarse_count * subs)
    owners = wide_count * narrow_count
    own_rows = subs // owners
    enc_sum, dec_sum, up_sum = lax.psum(
        (
            enc_total,
            dec_total,
            jnp.einsum(
                "kn,cn->kc", grad_rows, enc_flat, preferred_element_type=jnp.float32
            ).reshape(subs, fine_ch, chans),
        ),
        ("wide", "narrow"),
    )
    up_own = lax.dynamic_slice_in_dim(
        up_sum, lax.axis_index(("wide", "narrow")) * own_rows, own_rows, 0
    )
    return (
        grad_dark,
        unflatten(enc_sum) * coarse_scale,
        up_own * coarse_scale,
        unflatten(dec_sum) * fine_scale,
    )


def solution(mesh):
    in_specs = (P(None, None, "narrow", None), P(), P(), P(), P(None, "wide", "narrow", None))
    out_specs = (P(None, None, "narrow", None), P(), P(("wide", "narrow"), None, None), P())
    return jax.shard_map(
        on_device, mesh=mesh, in_specs=in_specs, out_specs=out_specs, check_vma=False
    )
```

profile of v0, /device:TPU:2, one launch (start us, length us, event | category | flops | bytes accessed | tf_op | source)
XLA Modules:
  0.0 539.2 jit_solution(12176044866597356027)
XLA Ops:
  7.2 5.1 collective-permute-start
  12.3 3.1 collective-permute-start.1
  18.8 3.0 copy.48
  30.1 2.0 concatenate.180
  33.5 2.0 concatenate.182
  36.8 2.0 concatenate.184
  40.2 2.0 concatenate.186
  44.7 2.7 convert_element_type.71
  47.4 3.5 copy.96
  67.7 4.2 collective-permute-start.4
  71.9 4.0 collective-permute-start.5
  85.5 3.3 collective-permute-start.6
  95.3 83.9 %psum.23 = f32[16,432]{1,0:T(8,128)S(1)} all-reduce(f32[16,432]{1,0:T(8,128)S(1)} %fusion.7), channel_id=1, replica_groups=mesh['wide'=32,'narrow'=8] {'wide','narrow'}, use_global_device_ids=true, to_apply=%region_2.3 | all-reduce | flops 6912 | bytes 55296 | tf_op jit(solution)/shard_map/psum | solution.py:173
  179.8 3.6 collective-permute-start.8
  183.4 4.6 collective-permute-start.9
  200.2 4.1 copy.70
  204.3 3.5 copy.65
  207.9 4.7 reshape.344
  213.0 33.9 %all-gather = bf16[64,512]{0,1:T(8,128)(2,1)S(1)} all-gather(bf16[64,16]{0,1:T(8,128)(2,1)S(1)} %fusion.10), channel_id=2, replica_groups=mesh['wide'=32,'narrow'=8] {'wide'}, dimensions={1}, use_global_device_ids=true | all-gather | bytes 67584 | tf_op jit(solution)/shard_map/all_gather | solution.py:159
  247.0 5.8 %collective-permute-start.10 = (bf16[64,32,1,16]{0,3,1,2:T(8,128)(2,1)S(1)}, bf16[64,32,1,16]{0,3,1,2:T(8,128)(2,1)S(1)}, u32[]{:S(2)}, u32[]{:S(2)}) collective-permute-start(bf16[64,32,1,16]{0,3,1,2:T(8,128)(2,1)S(1)} %fusion.37), channel_id=1, source_target_pairs={{0,1},{1,2},{2,3},{3,4},{4,5},{5,6},{6,7},{8,9},{9,10},{10,11},{11... | collective-permute-start | bytes 196616 | tf_op jit(solution)/shard_map/ppermute | solution.py:15
  252.9 2.6 collective-permute-start.11
  255.6 2.8 fusion.1
  259.5 2.3 collective-permute-done.11
  271.7 256.2 %all-reduce.8.cloned.1.call-done = (f32[64,1728]{1,0:T(8,128)}, f32[512,16,64]{2,0,1:T(8,128)}) async-done(((f32[64,1728]{1,0:T(8,128)}, f32[512,16,64]{2,0,1:T(8,128)}), (f32[64,1728]{1,0:T(8,128)}, f32[512,16,64]{2,0,1:T(8,128)})) %all-reduce.8.cloned.1.call-update) | async-done | bytes 2539536 | tf_op jit(solution)/shard_map/psum | solution.py:173
  (304 shorter events, 78.5 us)
Async XLA Ops:
  7.2 520.8 %all-reduce.8.cloned.1.call-start = ((), (), s32[]{:S(2)}) async-start(), calls=%async_computation | async-start | bytes 9306112 | tf_op jit(solution)/shard_map/psum | solution.py:173
  7.2 14.7 %collective-permute-start = (bf16[64,32,1,16]{0,3,1,2:T(8,128)(2,1)}, bf16[64,32,1,16]{0,3,1,2:T(8,128)(2,1)S(1)}, u32[]{:S(2)}, u32[]{:S(2)}) collective-permute-start(bf16[64,32,1,16]{0,3,1,2:T(8,128)(2,1)} %bitcast.228), channel_id=1, source_target_pairs={{0,1},{1,2},{2,3},{3,4},{4,5},{5,6},{6,7},{8,9},{9,10},{10,11},{11... | collective-permute-start | bytes 196616 | tf_op jit(solution)/shard_map/ppermute | solution.py:15
  12.3 10.2 %collective-permute-start.1 = (bf16[64,32,1,16]{0,3,1,2:T(8,128)(2,1)}, bf16[64,32,1,16]{0,3,1,2:T(8,128)(2,1)}, u32[]{:S(2)}, u32[]{:S(2)}) collective-permute-start(bf16[64,32,1,16]{0,3,1,2:T(8,128)(2,1)} %bitcast.229), channel_id=1, source_target_pairs={{1,0},{2,1},{3,2},{4,3},{5,4},{6,5},{7,6},{9,8},{10,9},{11,10},{12... | collective-permute-start | bytes 196616 | tf_op jit(solution)/shard_map/ppermute | solution.py:18
  27.7 5.8 %copy-start.24 = (bf16[64,8,1,16]{0,3,1,2:T(8,128)(2,1)S(1)}, bf16[64,8,1,16]{0,3,1,2:T(8,128)(2,1)}, u32[]{:S(2)}) copy-start(bf16[64,8,1,16]{0,3,1,2:T(8,128)(2,1)} %get-tuple-element.345) | copy-start | bytes 49156
  27.7 5.8 %copy-start.25 = (bf16[64,8,1,16]{0,3,1,2:T(8,128)(2,1)S(1)}, bf16[64,8,1,16]{0,3,1,2:T(8,128)(2,1)}, u32[]{:S(2)}) copy-start(bf16[64,8,1,16]{0,3,1,2:T(8,128)(2,1)} %get-tuple-element.346) | copy-start | bytes 49156
  27.7 5.8 %copy-start.26 = (bf16[64,8,1,16]{0,3,1,2:T(8,128)(2,1)S(1)}, bf16[64,8,1,16]{0,3,1,2:T(8,128)(2,1)}, u32[]{:S(2)}) copy-start(bf16[64,8,1,16]{0,3,1,2:T(8,128)(2,1)} %get-tuple-element.347) | copy-start | bytes 49156
  32.1 4.7 copy-start.22
  36.8 6.7 %copy-start.9 = (f32[64,8,1,16]{0,3,1,2:T(8,128)}, f32[64,8,1,16]{0,3,1,2:T(8,128)S(1)}, u32[]{:S(2)}) copy-start(f32[64,8,1,16]{0,3,1,2:T(8,128)S(1)} %convolution_bitcast_fusion.14) | copy-start | bytes 98308
  50.9 5.7 %copy-start.7 = (bf16[16,8,8,128]{3,2,1,0:T(8,128)(2,1)S(1)}, bf16[16,8,8,128]{3,2,1,0:T(8,128)(2,1)}, u32[]{:S(2)}) copy-start(bf16[16,8,8,128]{3,2,1,0:T(8,128)(2,1)} %param.9) | copy-start | bytes 786436
  53.5 12.9 %collective-permute-start.2 = (bf16[16,1,8,128]{3,0,2,1:T(8,128)(2,1)}, bf16[16,1,8,128]{3,0,2,1:T(8,128)(2,1)}, u32[]{:S(2)}, u32[]{:S(2)}) collective-permute-start(bf16[16,1,8,128]{3,0,2,1:T(8,128)(2,1)} %get-tuple-element.297), channel_id=1, source_target_pairs={{0,8},{8,16},{16,24},{24,32},{32,40},{40,48},{48,56},{56,64},{64,7... | collective-permute-start | bytes 98312 | tf_op jit(solution)/shard_map/ppermute | solution.py:15
  55.4 11.0 %collective-permute-start.3 = (bf16[16,1,8,128]{3,0,2,1:T(8,128)(2,1)}, bf16[16,1,8,128]{3,0,2,1:T(8,128)(2,1)S(1)}, u32[]{:S(2)}, u32[]{:S(2)}) collective-permute-start(bf16[16,1,8,128]{3,0,2,1:T(8,128)(2,1)} %get-tuple-element.298), channel_id=1, source_target_pairs={{8,0},{16,8},{24,16},{32,24},{40,32},{48,40},{56,48},{64,56},{72,6... | collective-permute-start | bytes 98312 | tf_op jit(solution)/shard_map/ppermute | solution.py:18
  67.7 10.6 %collective-permute-start.4 = (bf16[16,10,1,128]{3,0,2,1:T(8,128)(2,1)}, bf16[16,10,1,128]{3,0,2,1:T(8,128)(2,1)}, u32[]{:S(2)}, u32[]{:S(2)}) collective-permute-start(bf16[16,10,1,128]{3,0,2,1:T(8,128)(2,1)} %get-tuple-element.286), channel_id=1, source_target_pairs={{0,1},{1,2},{2,3},{3,4},{4,5},{5,6},{6,7},{8,9},{9,10},{10,11},{11... | collective-permute-start | bytes 122888 | tf_op jit(solution)/shard_map/ppermute | solution.py:15
  71.9 7.7 %collective-permute-start.5 = (bf16[16,10,1,128]{3,0,2,1:T(8,128)(2,1)}, bf16[16,10,1,128]{3,0,2,1:T(8,128)(2,1)}, u32[]{:S(2)}, u32[]{:S(2)}) collective-permute-start(bf16[16,10,1,128]{3,0,2,1:T(8,128)(2,1)} %get-tuple-element.287), channel_id=1, source_target_pairs={{1,0},{2,1},{3,2},{4,3},{5,4},{6,5},{7,6},{9,8},{10,9},{11,10},{12... | collective-permute-start | bytes 122888 | tf_op jit(solution)/shard_map/ppermute | solution.py:18
  85.5 4.7 collective-permute-start.6
  93.9 85.2 %collective-permute-start.7 = (bf16[16,1,8,128]{3,0,2,1:T(8,128)(2,1)S(1)}, bf16[16,1,8,128]{3,0,2,1:T(8,128)(2,1)S(1)}, u32[]{:S(2)}, u32[]{:S(2)}) collective-permute-start(bf16[16,1,8,128]{3,0,2,1:T(8,128)(2,1)S(1)} %slice.2150), channel_id=1, source_target_pairs={{8,0},{16,8},{24,16},{32,24},{40,32},{48,40},{56,48},{64,56},{72,6... | collective-permute-start | bytes 98312 | tf_op jit(solution)/shard_map/ppermute | solution.py:18
  179.8 10.6 %collective-permute-start.8 = (bf16[16,10,1,128]{3,0,2,1:T(8,128)(2,1)}, bf16[16,10,1,128]{3,0,2,1:T(8,128)(2,1)S(1)}, u32[]{:S(2)}, u32[]{:S(2)}) collective-permute-start(bf16[16,10,1,128]{3,0,2,1:T(8,128)(2,1)} %get-tuple-element.282), channel_id=1, source_target_pairs={{0,1},{1,2},{2,3},{3,4},{4,5},{5,6},{6,7},{8,9},{9,10},{10,11},{11... | collective-permute-start | bytes 122888 | tf_op jit(solution)/shard_map/ppermute | solution.py:15
  183.4 7.6 %collective-permute-start.9 = (bf16[16,10,1,128]{3,0,2,1:T(8,128)(2,1)}, bf16[16,10,1,128]{3,0,2,1:T(8,128)(2,1)S(1)}, u32[]{:S(2)}, u32[]{:S(2)}) collective-permute-start(bf16[16,10,1,128]{3,0,2,1:T(8,128)(2,1)} %get-tuple-element.283), channel_id=1, source_target_pairs={{1,0},{2,1},{3,2},{4,3},{5,4},{6,5},{7,6},{9,8},{10,9},{11,10},{12... | collective-permute-start | bytes 122888 | tf_op jit(solution)/shard_map/ppermute | solution.py:18
  212.6 34.4 %copy-start.10 = (f32[64,8,1,16]{0,3,1,2:T(8,128)S(1)}, f32[64,8,1,16]{0,3,1,2:T(8,128)}, u32[]{:S(2)}) copy-start(f32[64,8,1,16]{0,3,1,2:T(8,128)} %copy-done.9) | copy-start | bytes 98308
  212.6 34.4 %copy-start.12 = (f32[64,8,1,16]{0,3,1,2:T(8,128)S(1)}, f32[64,8,1,16]{0,3,1,2:T(8,128)}, u32[]{:S(2)}) copy-start(f32[64,8,1,16]{0,3,1,2:T(8,128)} %copy-done.11) | copy-start | bytes 98308
  212.6 34.3 %copy-start.14 = (f32[64,8,1,16]{0,3,1,2:T(8,128)S(1)}, f32[64,8,1,16]{0,3,1,2:T(8,128)}, u32[]{:S(2)}) copy-start(f32[64,8,1,16]{0,3,1,2:T(8,128)} %copy-done.13) | copy-start | bytes 98308
  212.6 42.9 %copy-start = (bf16[8,8,8,16,1,1,16]{6,3,2,1,0,5,4:T(8,128)(2,1)S(1)}, bf16[8,8,8,16,1,1,16]{6,3,2,1,0,5,4:T(8,128)(2,1)}, u32[]{:S(2)}) copy-start(bf16[8,8,8,16,1,1,16]{6,3,2,1,0,5,4:T(8,128)(2,1)} %copy.70) | copy-start | bytes 786436
  212.6 42.9 %copy-start.6 = (bf16[64,32,1,16]{0,3,1,2:T(8,128)(2,1)S(1)}, bf16[64,32,1,16]{0,3,1,2:T(8,128)(2,1)}, u32[]{:S(2)}) copy-start(bf16[64,32,1,16]{0,3,1,2:T(8,128)(2,1)} %copy-done.5) | copy-start | bytes 196612
  247.0 12.4 %collective-permute-start.10 = (bf16[64,32,1,16]{0,3,1,2:T(8,128)(2,1)S(1)}, bf16[64,32,1,16]{0,3,1,2:T(8,128)(2,1)S(1)}, u32[]{:S(2)}, u32[]{:S(2)}) collective-permute-start(bf16[64,32,1,16]{0,3,1,2:T(8,128)(2,1)S(1)} %fusion.37), channel_id=1, source_target_pairs={{0,1},{1,2},{2,3},{3,4},{4,5},{5,6},{6,7},{8,9},{9,10},{10,11},{11... | collective-permute-start | bytes 196616 | tf_op jit(solution)/shard_map/ppermute | solution.py:15
  252.9 8.9 %collective-permute-start.11 = (bf16[64,32,1,16]{0,3,1,2:T(8,128)(2,1)S(1)}, bf16[64,32,1,16]{0,3,1,2:T(8,128)(2,1)S(1)}, u32[]{:S(2)}, u32[]{:S(2)}) collective-permute-start(bf16[64,32,1,16]{0,3,1,2:T(8,128)(2,1)S(1)} %fusion.37), channel_id=1, source_target_pairs={{1,0},{2,1},{3,2},{4,3},{5,4},{6,5},{7,6},{9,8},{10,9},{11,10},{12... | collective-permute-start | bytes 196616 | tf_op jit(solution)/shard_map/ppermute | solution.py:18
  (16 other events, 38.0 us)
Sparse Core Ops, SparseCore 0:
  259.6 268.3 all-reduce.7
where the time goes:
time: 542 us; the launch traced here: 539 us
  waiting for transfers between devices  261 us (48%)
  blocking collectives  118 us (22%)
  local copies, waits for them, and re-layouts  76.8 us (14%)
  starting transfers between devices  41 us (8%)
  matrix products  16.3 us (3%)
  between operations  15.5 us (3%)
  other arithmetic  11.2 us (2%)
    psum x1, waiting for transfers between devices, on_device(): lax.psum((enc_total, dec_total, jnp.einsum('kn,cn->kc', grad_rows, enc_fl...  256 us
    psum x1, blocking collectives, on_device(): lax.psum((enc_total, dec_total, jnp.einsum('kn,cn->kc', grad_rows, enc_fl...  83.9 us
    all_gather x1, blocking collectives, on_device(): enc_grad = lax.all_gather(enc_grad_own, 'wide', axis=1, tiled=True)  33.9 us
    ppermute x6, starting transfers between devices, padded_2(): lax.ppermute(lax.slice_in_dim(block, block.shape[dim] - width, None, axis...  24 us
    ppermute x6, starting transfers between devices, padded_2(): lax.ppermute(lax.slice_in_dim(block, 0, width, axis=dim), axis, backward)  17.1 us
    concatenate x15, local copies, waits for them, and re-layouts, columns(): return jnp.concatenate(pieces, 0)  15.1 us
    unnamed x175, local copies, waits for them, and re-layouts  14.7 us
    slice x17, local copies, waits for them, and re-layouts, columns(): padded[:, first + shift_x:first + shift_x + count, shift_z:shift_z + dept...  11.8 us
  transfers between devices with their start and end apart: 13, of which 4 were waited for; matrix products, arithmetic and copies ran while one was open for 7% of the time, Pallas kernels for 0%

commit v1 on v0

--- a/solution.py
+++ b/solution.py
@@ -5,6 +5,15 @@
 from jax.sharding import PartitionSpec as P
 
 RATIO = 8
+get_gates = lambda sample: jnp.concatenate(
+    lax.all_to_all(
+        jnp.stack([sample for _ in range(lax.psum(1, axis_name="wide"))], 0),
+        axis_name="wide",
+        concat_axis=0,
+        split_axis=0,
+    ),
+    axis=1,
+)
 
 
 def padded_2(block, sides, width):
@@ -156,7 +165,7 @@
         .reshape(chans, own_planes, depth, width)
         .astype(jnp.bfloat16)
     )
-    enc_grad = lax.all_gather(enc_grad_own, "wide", axis=1, tiled=True)
+    enc_grad = get_gates(enc_grad_own)
     enc_pre_grad = (enc_grad.astype(jnp.float32) * silu_slope(enc_pre)).astype(jnp.bfloat16)
     grad_own = lax.dynamic_slice_in_dim(enc_pre_grad, first_plane, own_planes, 1)
     dark_own = lax.dynamic_slice_in_dim(dark_padded, first_plane, own_planes + 2, 1)

time: 542 us -> 522 us (0.963)
  blocking collectives: 118 us -> 83.9 us
  starting transfers between devices: 41 us -> 47.9 us
    all_gather x1 -> x0, blocking collectives: 33.9 us -> none  [on_device(): enc_grad = lax.all_gather(enc_grad_own, 'wide', axis=1, tiled=True)]
    all_to_all x0 -> x1, starting transfers between devices: none -> 6.87 us  [lax.all_to_all(jnp.stack([sample for _ in range(lax.psum(1, axis_name='wi...]
    unnamed x175 -> x194, local copies, waits for them, and re-layouts: 14.7 us -> 15.2 us
  transfers between devices with their start and end apart: 13 -> 14, of which waited for: 4 -> 5; matrix products, arithmetic and copies ran while one was open for 7% -> 7% of each run, Pallas kernels for 0% -> 0%
where the time goes in v1:
time: 522 us; the launch traced here: 519 us
  waiting for transfers between devices  266 us (51%)
  blocking collectives  83.9 us (16%)
  local copies, waits for them, and re-layouts  76.8 us (15%)
  starting transfers between devices  47.9 us (9%)
  matrix products  18 us (3%)
  between operations  15.6 us (3%)
  other arithmetic  11.2 us (2%)
    psum x1, waiting for transfers between devices, on_device(): lax.psum((enc_total, dec_total, jnp.einsum('kn,cn->kc', grad_rows, enc_fl...  255 us
    psum x1, blocking collectives, on_device(): lax.psum((enc_total, dec_total, jnp.einsum('kn,cn->kc', grad_rows, enc_fl...  83.9 us
    ppermute x6, starting transfers between devices, padded_2(): lax.ppermute(lax.slice_in_dim(block, block.shape[dim] - width, None, axis...  23.9 us
    ppermute x6, starting transfers between devices, padded_2(): lax.ppermute(lax.slice_in_dim(block, 0, width, axis=dim), axis, backward)  16.8 us
    unnamed x194, local copies, waits for them, and re-layouts  15.2 us
    concatenate x15, local copies, waits for them, and re-layouts, columns(): return jnp.concatenate(pieces, 0)  14.5 us
    slice x17, local copies, waits for them, and re-layouts, columns(): padded[:, first + shift_x:first + shift_x + count, shift_z:shift_z + dept...  12 us
  transfers between devices with their start and end apart: 14, of which 5 were waited for; matrix products, arithmetic and copies ran while one was open for 7% of the time, Pallas kernels for 0%

profile of v1, /device:TPU:2, one launch (start us, length us, event | category | flops | bytes accessed | tf_op | source)
XLA Modules:
  0.0 519.5 jit_solution(11381158895782061075)
XLA Ops:
  7.2 5.1 collective-permute-start
  12.3 3.1 collective-permute-start.1
  18.8 3.0 copy.91
  30.1 2.0 concatenate.180
  33.6 2.0 concatenate.182
  37.0 2.0 concatenate.184
  44.4 2.7 convert_element_type.91
  47.1 3.5 copy.140
  67.3 4.2 collective-permute-start.4
  71.5 4.0 collective-permute-start.5
  85.2 3.3 collective-permute-start.6
  94.9 83.9 %psum.23 = f32[16,432]{1,0:T(8,128)S(1)} all-reduce(f32[16,432]{1,0:T(8,128)S(1)} %fusion.7), channel_id=1, replica_groups=mesh['wide'=32,'narrow'=8] {'wide','narrow'}, use_global_device_ids=true, to_apply=%region_2.3 | all-reduce | flops 6912 | bytes 55296 | tf_op jit(solution)/shard_map/psum | solution.py:182
  179.5 3.6 collective-permute-start.8
  183.1 4.6 collective-permute-start.9
  199.9 4.1 copy.114
  204.0 3.5 copy.108
  207.5 4.7 reshape.371
  213.4 6.9 %all-to-all-start = ((bf16[32,2,512]{2,1,0:T(2,128)(2,1)}), bf16[32,2,512]{2,1,0:T(2,128)(2,1)S(1)}, u32[]{:S(2)}, u32[]{:S(2)}) async-start(bf16[32,2,512]{2,1,0:T(2,128)(2,1)} %reshape.395), calls=%async_computation | async-start | bytes 131072 | tf_op jit(solution)/shard_map/all_to_all | solution.py:9
  220.6 4.5 fusion.1
  225.1 4.3 all-to-all-done
  229.6 5.8 %collective-permute-start.10 = (bf16[64,32,1,16]{0,3,1,2:T(8,128)(2,1)S(1)}, bf16[64,32,1,16]{0,3,1,2:T(8,128)(2,1)S(1)}, u32[]{:S(2)}, u32[]{:S(2)}) collective-permute-start(bf16[64,32,1,16]{0,3,1,2:T(8,128)(2,1)S(1)} %fusion.37), channel_id=1, source_target_pairs={{0,1},{1,2},{2,3},{3,4},{4,5},{5,6},{6,7},{8,9},{9,10},{10,11},{11... | collective-permute-start | bytes 196616 | tf_op jit(solution)/shard_map/ppermute | solution.py:24
  235.5 2.4 collective-permute-start.11
  239.0 4.8 collective-permute-done.11
  253.4 254.9 %all-reduce.8.cloned.1.call-done = (f32[64,1728]{1,0:T(8,128)}, f32[512,16,64]{2,0,1:T(8,128)}) async-done(((f32[64,1728]{1,0:T(8,128)}, f32[512,16,64]{2,0,1:T(8,128)}), (f32[64,1728]{1,0:T(8,128)}, f32[512,16,64]{2,0,1:T(8,128)})) %all-reduce.8.cloned.1.call-update) | async-done | bytes 2539536 | tf_op jit(solution)/shard_map/psum | solution.py:182
  (324 shorter events, 80.8 us)
Async XLA Ops:
  7.2 14.7 %collective-permute-start = (bf16[64,32,1,16]{0,3,1,2:T(8,128)(2,1)}, bf16[64,32,1,16]{0,3,1,2:T(8,128)(2,1)S(1)}, u32[]{:S(2)}, u32[]{:S(2)}) collective-permute-start(bf16[64,32,1,16]{0,3,1,2:T(8,128)(2,1)} %bitcast.238), channel_id=1, source_target_pairs={{0,1},{1,2},{2,3},{3,4},{4,5},{5,6},{6,7},{8,9},{9,10},{10,11},{11... | collective-permute-start | bytes 196616 | tf_op jit(solution)/shard_map/ppermute | solution.py:24
  12.3 10.2 %collective-permute-start.1 = (bf16[64,32,1,16]{0,3,1,2:T(8,128)(2,1)}, bf16[64,32,1,16]{0,3,1,2:T(8,128)(2,1)}, u32[]{:S(2)}, u32[]{:S(2)}) collective-permute-start(bf16[64,32,1,16]{0,3,1,2:T(8,128)(2,1)} %bitcast.239), channel_id=1, source_target_pairs={{1,0},{2,1},{3,2},{4,3},{5,4},{6,5},{7,6},{9,8},{10,9},{11,10},{12... | collective-permute-start | bytes 196616 | tf_op jit(solution)/shard_map/ppermute | solution.py:27
  27.7 5.8 %copy-start.27 = (bf16[64,8,1,16]{0,3,1,2:T(8,128)(2,1)S(1)}, bf16[64,8,1,16]{0,3,1,2:T(8,128)(2,1)}, u32[]{:S(2)}) copy-start(bf16[64,8,1,16]{0,3,1,2:T(8,128)(2,1)} %get-tuple-element.349) | copy-start | bytes 49156
  27.7 5.8 %copy-start.28 = (bf16[64,8,1,16]{0,3,1,2:T(8,128)(2,1)S(1)}, bf16[64,8,1,16]{0,3,1,2:T(8,128)(2,1)}, u32[]{:S(2)}) copy-start(bf16[64,8,1,16]{0,3,1,2:T(8,128)(2,1)} %get-tuple-element.350) | copy-start | bytes 49156
  27.7 5.8 %copy-start.29 = (bf16[64,8,1,16]{0,3,1,2:T(8,128)(2,1)S(1)}, bf16[64,8,1,16]{0,3,1,2:T(8,128)(2,1)}, u32[]{:S(2)}) copy-start(bf16[64,8,1,16]{0,3,1,2:T(8,128)(2,1)} %get-tuple-element.351) | copy-start | bytes 49156
  36.9 6.7 %copy-start.8 = (f32[64,8,1,16]{0,3,1,2:T(8,128)}, f32[64,8,1,16]{0,3,1,2:T(8,128)S(1)}, u32[]{:S(2)}) copy-start(f32[64,8,1,16]{0,3,1,2:T(8,128)S(1)} %convolution_bitcast_fusion.14) | copy-start | bytes 98308
  50.6 5.7 %copy-start.6 = (bf16[16,8,8,128]{3,2,1,0:T(8,128)(2,1)S(1)}, bf16[16,8,8,128]{3,2,1,0:T(8,128)(2,1)}, u32[]{:S(2)}) copy-start(bf16[16,8,8,128]{3,2,1,0:T(8,128)(2,1)} %param.9) | copy-start | bytes 786436
  53.1 12.9 %collective-permute-start.2 = (bf16[16,1,8,128]{3,0,2,1:T(8,128)(2,1)}, bf16[16,1,8,128]{3,0,2,1:T(8,128)(2,1)}, u32[]{:S(2)}, u32[]{:S(2)}) collective-permute-start(bf16[16,1,8,128]{3,0,2,1:T(8,128)(2,1)} %get-tuple-element.301), channel_id=1, source_target_pairs={{0,8},{8,16},{16,24},{24,32},{32,40},{40,48},{48,56},{56,64},{64,7... | collective-permute-start | bytes 98312 | tf_op jit(solution)/shard_map/ppermute | solution.py:24
  55.0 11.0 %collective-permute-start.3 = (bf16[16,1,8,128]{3,0,2,1:T(8,128)(2,1)}, bf16[16,1,8,128]{3,0,2,1:T(8,128)(2,1)S(1)}, u32[]{:S(2)}, u32[]{:S(2)}) collective-permute-start(bf16[16,1,8,128]{3,0,2,1:T(8,128)(2,1)} %get-tuple-element.302), channel_id=1, source_target_pairs={{8,0},{16,8},{24,16},{32,24},{40,32},{48,40},{56,48},{64,56},{72,6... | collective-permute-start | bytes 98312 | tf_op jit(solution)/shard_map/ppermute | solution.py:27
  67.3 10.5 %collective-permute-start.4 = (bf16[16,10,1,128]{3,0,2,1:T(8,128)(2,1)}, bf16[16,10,1,128]{3,0,2,1:T(8,128)(2,1)}, u32[]{:S(2)}, u32[]{:S(2)}) collective-permute-start(bf16[16,10,1,128]{3,0,2,1:T(8,128)(2,1)} %get-tuple-element.290), channel_id=1, source_target_pairs={{0,1},{1,2},{2,3},{3,4},{4,5},{5,6},{6,7},{8,9},{9,10},{10,11},{11... | collective-permute-start | bytes 122888 | tf_op jit(solution)/shard_map/ppermute | solution.py:24
  71.5 7.7 %collective-permute-start.5 = (bf16[16,10,1,128]{3,0,2,1:T(8,128)(2,1)}, bf16[16,10,1,128]{3,0,2,1:T(8,128)(2,1)}, u32[]{:S(2)}, u32[]{:S(2)}) collective-permute-start(bf16[16,10,1,128]{3,0,2,1:T(8,128)(2,1)} %get-tuple-element.291), channel_id=1, source_target_pairs={{1,0},{2,1},{3,2},{4,3},{5,4},{6,5},{7,6},{9,8},{10,9},{11,10},{12... | collective-permute-start | bytes 122888 | tf_op jit(solution)/shard_map/ppermute | solution.py:27
  85.2 4.7 collective-permute-start.6
  93.6 85.2 %collective-permute-start.7 = (bf16[16,1,8,128]{3,0,2,1:T(8,128)(2,1)S(1)}, bf16[16,1,8,128]{3,0,2,1:T(8,128)(2,1)S(1)}, u32[]{:S(2)}, u32[]{:S(2)}) collective-permute-start(bf16[16,1,8,128]{3,0,2,1:T(8,128)(2,1)S(1)} %slice.2150), channel_id=1, source_target_pairs={{8,0},{16,8},{24,16},{32,24},{40,32},{48,40},{56,48},{64,56},{72,6... | collective-permute-start | bytes 98312 | tf_op jit(solution)/shard_map/ppermute | solution.py:27
  179.5 10.6 %collective-permute-start.8 = (bf16[16,10,1,128]{3,0,2,1:T(8,128)(2,1)}, bf16[16,10,1,128]{3,0,2,1:T(8,128)(2,1)S(1)}, u32[]{:S(2)}, u32[]{:S(2)}) collective-permute-start(bf16[16,10,1,128]{3,0,2,1:T(8,128)(2,1)} %get-tuple-element.286), channel_id=1, source_target_pairs={{0,1},{1,2},{2,3},{3,4},{4,5},{5,6},{6,7},{8,9},{9,10},{10,11},{11... | collective-permute-start | bytes 122888 | tf_op jit(solution)/shard_map/ppermute | solution.py:24
  183.1 7.6 %collective-permute-start.9 = (bf16[16,10,1,128]{3,0,2,1:T(8,128)(2,1)}, bf16[16,10,1,128]{3,0,2,1:T(8,128)(2,1)S(1)}, u32[]{:S(2)}, u32[]{:S(2)}) collective-permute-start(bf16[16,10,1,128]{3,0,2,1:T(8,128)(2,1)} %get-tuple-element.287), channel_id=1, source_target_pairs={{1,0},{2,1},{3,2},{4,3},{5,4},{6,5},{7,6},{9,8},{10,9},{11,10},{12... | collective-permute-start | bytes 122888 | tf_op jit(solution)/shard_map/ppermute | solution.py:27
  212.2 8.4 %copy-start.5 = (bf16[64,32,1,16]{0,3,1,2:T(8,128)(2,1)S(1)}, bf16[64,32,1,16]{0,3,1,2:T(8,128)(2,1)}, u32[]{:S(2)}) copy-start(bf16[64,32,1,16]{0,3,1,2:T(8,128)(2,1)} %copy-done.4) | copy-start | bytes 196612
  213.4 15.9 %all-to-all-start = ((bf16[32,2,512]{2,1,0:T(2,128)(2,1)}), bf16[32,2,512]{2,1,0:T(2,128)(2,1)S(1)}, u32[]{:S(2)}, u32[]{:S(2)}) async-start(bf16[32,2,512]{2,1,0:T(2,128)(2,1)} %reshape.395), calls=%async_computation | async-start | bytes 131072 | tf_op jit(solution)/shard_map/all_to_all | solution.py:9
  220.3 288.0 %all-reduce.8.cloned.1.call-start = ((), (), s32[]{:S(2)}) async-start(), calls=%async_computation.1 | async-start | bytes 9306112 | tf_op jit(solution)/shard_map/psum | solution.py:182
  220.6 8.9 %copy-start.9 = (f32[64,8,1,16]{0,3,1,2:T(8,128)S(1)}, f32[64,8,1,16]{0,3,1,2:T(8,128)}, u32[]{:S(2)}) copy-start(f32[64,8,1,16]{0,3,1,2:T(8,128)} %copy-done.8) | copy-start | bytes 98308
  220.6 8.9 %copy-start.11 = (f32[64,8,1,16]{0,3,1,2:T(8,128)S(1)}, f32[64,8,1,16]{0,3,1,2:T(8,128)}, u32[]{:S(2)}) copy-start(f32[64,8,1,16]{0,3,1,2:T(8,128)} %copy-done.10) | copy-start | bytes 98308
  220.6 8.9 %copy-start.13 = (f32[64,8,1,16]{0,3,1,2:T(8,128)S(1)}, f32[64,8,1,16]{0,3,1,2:T(8,128)}, u32[]{:S(2)}) copy-start(f32[64,8,1,16]{0,3,1,2:T(8,128)} %copy-done.12) | copy-start | bytes 98308
  220.6 17.3 %copy-start.15 = (bf16[1728,1,1,16]{0,3,1,2:T(8,128)(2,1)S(1)}, bf16[1728,1,1,16]{0,3,1,2:T(8,128)(2,1)}, u32[]{:S(2)}) copy-start(bf16[1728,1,1,16]{0,3,1,2:T(8,128)(2,1)} %concatenate.219) | copy-start | bytes 165892
  229.6 9.4 %collective-permute-start.10 = (bf16[64,32,1,16]{0,3,1,2:T(8,128)(2,1)S(1)}, bf16[64,32,1,16]{0,3,1,2:T(8,128)(2,1)S(1)}, u32[]{:S(2)}, u32[]{:S(2)}) collective-permute-start(bf16[64,32,1,16]{0,3,1,2:T(8,128)(2,1)S(1)} %fusion.37), channel_id=1, source_target_pairs={{0,1},{1,2},{2,3},{3,4},{4,5},{5,6},{6,7},{8,9},{9,10},{10,11},{11... | collective-permute-start | bytes 196616 | tf_op jit(solution)/shard_map/ppermute | solution.py:24
  235.5 8.4 %collective-permute-start.11 = (bf16[64,32,1,16]{0,3,1,2:T(8,128)(2,1)S(1)}, bf16[64,32,1,16]{0,3,1,2:T(8,128)(2,1)S(1)}, u32[]{:S(2)}, u32[]{:S(2)}) collective-permute-start(bf16[64,32,1,16]{0,3,1,2:T(8,128)(2,1)S(1)} %fusion.37), channel_id=1, source_target_pairs={{1,0},{2,1},{3,2},{4,3},{5,4},{6,5},{7,6},{9,8},{10,9},{11,10},{12... | collective-permute-start | bytes 196616 | tf_op jit(solution)/shard_map/ppermute | solution.py:27
  (25 other events, 78.6 us)
Sparse Core Ops, SparseCore 0:
  239.1 269.1 all-reduce.7
